TPU v7x, 32 devices: a whole 2x2x4 slice. The times are simulated.
32 devices in a mesh: chain: 4 (over x, core), band: 8 (over z, y).
Axes of the slice: x: 2, y: 2, z: 4, core: 2. Of those that a mesh axis runs over, the one named last changes fastest.
Arguments:
- diag_inverse: float32 [8192, 2048], P(('chain', 'band'))
- coupling: float32 [8192, 2048], P('chain', 'band'), may hold values from -0.09375 to 0.09375
- elem_stiff: float32 [24, 24, 16384], P(None, None, ('chain', 'band')), may hold values from -6 to 6
- elem_mass: float32 [24, 24, 16384], P(None, None, ('chain', 'band')), may hold values from -6 to 6
- elem_dofs: int32 [24, 16384], P(None, ('chain', 'band')), may hold values from 0 to 2047
- elem_slab: int32 [16384, 1], P(('chain', 'band')), may hold values from 0 to 3; in each aligned block of 512 rows (0 to 511, 512 to 1023, ...) at most 256 rows name the same one
- elem_var: int32 [16384], P(('chain', 'band')), may hold values from 0 to 191
- mode: float32 [8192], P(('chain', 'band')), may hold values from -0.4 to 0.4
- mass_mode: float32 [8192], P('chain'), may hold values from -1.2 to 1.2
- eigenvalue: float32 [1], replicated, may hold values from 0.5 to 2
Outputs:
- eigvec_slope: float32 [192, 8192], P(None, ('chain', 'band'))
- eigval_slope: float32 [192], replicated
Inputs may be any that keep to these rules, and one draw needn't show every extreme that they name: `elem_slab`: within the rows of one device no slab is named by more than 256 elements, a bound that some block reaches.
All inputs are finite; a program needn't handle non-finite values.
Results may differ from a plain program's by a relative error of at most 0.00014.
Values sent between devices are 32-bit elements; how exact they have to be, the bound alone decides.
No kernel may reach another device: no remote copies, remote signals or barrier semaphores. Data moves between devices by JAX's collectives and lax.ppermute only.
A program may use at most 64 MiB of HBM per device.

v0:
```python
import jax
import jax.numpy as jnp
from jax import lax
from jax.sharding import PartitionSpec as P

VARS = 192
PANELS = 4


def from_behind(value, axis, by):
    size = lax.axis_size(axis)
    pairs = [(i, i + by) for i in range(size) if 0 <= i + by < size]
    return lax.ppermute(value, axis, pairs)


def sweep(stored, shift_by, iterations, panel_rows, piece_cols, prepare, finish):

    def advance(iteration, carry):
        outgoing, kept = carry
        received = from_behind(outgoing, "chain", shift_by)
        partial_value, context = prepare(iteration, received, kept)
        summed = lax.psum(partial_value, "band")
        return finish(iteration, summed, context, kept)

    outgoing = jnp.zeros((panel_rows, piece_cols), jnp.float32)
    return lax.fori_loop(0, iterations, advance, (outgoing, stored))[1]


def on_device(
    diag_inverse,
    coupling,
    elem_stiff,
    elem_mass,
    elem_dofs,
    elem_slab,
    elem_var,
    mode,
    mass_mode,
    eigenvalue,
):
    highest = lax.Precision.HIGHEST
    chain_len = lax.axis_size("chain")
    chain_pos = lax.axis_index("chain")
    band_pos = lax.axis_index("band")
    piece_cols = diag_inverse.shape[0]
    slab_rows = diag_inverse.shape[1]
    elem_width = elem_dofs.shape[0]
    elem_count = elem_dofs.shape[1]
    capacity = 2 * elem_count // chain_len
    eigen_val = eigenvalue[0]
    whole_mode = lax.all_gather(mode, ("chain", "band"), axis=0, tiled=True)
    dest_slab = elem_slab[:, 0]
    dof_index = dest_slab[None, :] * slab_rows + elem_dofs
    mode_at = whole_mode[dof_index]
    operator = elem_stiff - eigen_val * elem_mass
    loads = -jnp.einsum("ije,je->ie", operator, mode_at, precision=highest)
    quadratic = -jnp.sum(mode_at * loads, axis=0)
    matches = (elem_var[None, :] == jnp.arange(VARS)[:, None]).astype(jnp.float32)
    local_slope = jnp.dot(matches, quadratic, precision=highest)
    eigval_slope = lax.psum(local_slope, ("chain", "band"))
    onehot = (dest_slab[:, None] == jnp.arange(chain_len)[None, :]).astype(jnp.int32)
    slot_rank = jnp.sum((jnp.cumsum(onehot, axis=0) - 1) * onehot, axis=1)
    flat_index = elem_var[None, :] * slab_rows + elem_dofs
    send_values = (
        jnp.zeros((chain_len, elem_width, capacity), jnp.float32)
        .at[dest_slab, :, slot_rank]
        .set(loads.T)
    )
    send_index = (
        jnp.zeros((chain_len, elem_width, capacity), jnp.int32)
        .at[dest_slab, :, slot_rank]
        .set(flat_index.T)
    )
    got_values, got_index = (
        lax.all_to_all(send_values, "chain", split_axis=0, concat_axis=0, tiled=True),
        lax.all_to_all(send_index, "chain", split_axis=0, concat_axis=0, tiled=True),
    )
    assembled = (
        jnp.zeros((VARS * slab_rows,), jnp.float32)
        .at[got_index.reshape(-1)]
        .add(got_values.reshape(-1))
    )
    assembled = assembled.reshape(VARS, slab_rows)
    slope_term = eigval_slope[:, None] * mass_mode[None, :]
    panel_count = PANELS
    panel_rows = VARS // panel_count
    iterations = chain_len + panel_count - 1
    contract = (((1,), (1,)), ((), ()))

    def locate(panel_index):
        active = (panel_index >= 0) & (panel_index < panel_count)
        first_row = jnp.clip(panel_index, 0, panel_count - 1) * panel_rows
        return (active, first_row)

    def place(kept, fresh, active, first_row):
        previous = lax.dynamic_slice_in_dim(kept, first_row, panel_rows, 0)
        return lax.dynamic_update_slice_in_dim(
            kept, jnp.where(active, fresh, previous), first_row, 0
        )

    def forward_prepare(iteration, received, kept):
        active, first_row = locate(iteration - chain_pos)
        rhs_panel = lax.dynamic_slice_in_dim(assembled, first_row, panel_rows, 0)
        carried = lax.dot_general(
            received, coupling, contract, precision=highest, preferred_element_type=jnp.float32
        )
        return (rhs_panel - carried, (active, first_row))

    def forward_finish(iteration, summed, context, kept):
        active, first_row = context
        coupled = summed + lax.dynamic_slice_in_dim(slope_term, first_row, panel_rows, 0)
        fresh = lax.dot_general(
            coupled, diag_inverse, contract, precision=highest, preferred_element_type=jnp.float32
        )
        return (fresh, place(kept, fresh, active, first_row))

    forward_kept = sweep(
        jnp.zeros((VARS, piece_cols), jnp.float32),
        1,
        iterations,
        panel_rows,
        piece_cols,
        forward_prepare,
        forward_finish,
    )

    def backward_prepare(iteration, received, kept):
        active, first_row = locate(iteration - (chain_len - 1 - chain_pos))
        remain = lax.dynamic_slice_in_dim(forward_kept, first_row, panel_rows, 0) - received
        partial_value = jnp.dot(
            remain, diag_inverse, precision=highest, preferred_element_type=jnp.float32
        )
        return (partial_value, (active, first_row))

    def backward_finish(iteration, summed, context, kept):
        active, first_row = context
        own_piece = lax.dynamic_slice_in_dim(summed, band_pos * piece_cols, piece_cols, 1)
        outgoing = jnp.dot(summed, coupling, precision=highest, preferred_element_type=jnp.float32)
        return (outgoing, place(kept, own_piece, active, first_row))

    eigvec_slope = sweep(
        jnp.zeros((VARS, piece_cols), jnp.float32),
        -1,
        iterations,
        panel_rows,
        piece_cols,
        backward_prepare,
        backward_finish,
    )
    return (eigvec_slope, eigval_slope)


def solution(mesh):
    in_specs = (
        P(("chain", "band"), None),
        P("chain", "band"),
        P(None, None, ("chain", "band")),
        P(None, None, ("chain", "band")),
        P(None, ("chain", "band")),
        P(("chain", "band"), None),
        P(("chain", "band")),
        P(("chain", "band")),
        P("chain"),
        P(),
    )
    out_specs = (P(None, ("chain", "band")), P())
    return jax.shard_map(
        on_device, mesh=mesh, in_specs=in_specs, out_specs=out_specs, check_vma=False
    )
```

profile of v0, /device:TPU:0, one launch (start us, length us, event | category | flops | bytes accessed | tf_op | source)
XLA Modules:
  0.0 1582.4 jit_solution(5994299352049603090)
XLA Ops:
  8.7 70.1 %all-gather = f32[32,1,256]{2,1,0:T(1,128)S(1)} all-gather(f32[1,1,256]{2,1,0:T(1,128)} %bitcast.73), channel_id=1, replica_groups=mesh['chain'=4,'band'=8] {'chain','band'}, dimensions={0}, use_global_device_ids=true | all-gather | bytes 33792 | tf_op jit(solution)/shard_map/all_gather | solution.py:51
  78.8 68.0 %gather_fusion = f32[12288]{0:T(1024)S(1)} fusion(f32[8192]{0:T(1024)S(1)} %bitcast.59, s32[12288]{0:T(1024)S(1)} %broadcast_clamp_fusion), kind=kCustom, calls=%fused_computation | custom fusion | bytes 147456 | tf_op jit(solution)/shard_map/gather | solution.py:54
  149.9 24.8 %scatter_fusion.1 = f32[4,24,256]{1,2,0:T(8,128)S(1)} fusion(f32[4,24,256]{1,2,0:T(8,128)S(1)} %broadcast_in_dim.10, s32[512]{0:T(512)S(1)} %bitcast.60, f32[512,24]{1,0:T(8,128)S(1)} %copy.19), kind=kCustom, calls=%fused_computation.2 | custom fusion | bytes 151552 | tf_op jit(solution)/shard_map/scatter | solution.py:67
  175.5 3.4 all-to-all-start.1
  179.5 24.8 %scatter_fusion = s32[4,24,256]{1,2,0:T(8,128)S(1)} fusion(s32[4,24,256]{1,2,0:T(8,128)S(1)} %broadcast_in_dim.9, s32[512]{0:T(512)S(1)} %bitcast.61, s32[512,24]{1,0:T(8,128)S(1)} %copy.17), kind=kCustom, calls=%fused_computation.1 | custom fusion | bytes 151552 | tf_op jit(solution)/shard_map/scatter | solution.py:72
  205.2 36.8 %psum.31 = f32[192]{0:T(256)S(1)} all-reduce(f32[192]{0:T(256)S(1)} %bitcast.74), channel_id=1, replica_groups=mesh['chain'=4,'band'=8] {'chain','band'}, use_global_device_ids=true, to_apply=%region_7.8 | all-reduce | flops 192 | bytes 1536 | tf_op jit(solution)/shard_map/psum | solution.py:60
  242.0 3.5 all-to-all-start
  245.5 1.3 broadcast_multiply_fusion
  246.9 2.9 all-to-all-done
  250.0 157.2 %scatter_custom_fusion.2 = f32[393216]{0:T(1024)} fusion(s32[24576]{0:T(1024)S(1)} %bitcast.66, f32[24576]{0:T(1024)S(1)} %bitcast.65, f32[]{:T(128)} %constant.139.clone.1), kind=kCustom, calls=%fused_computation.17 | custom fusion | flops 24576 | bytes 1572868 | tf_op jit(solution)/shard_map/scatter-add | solution.py:81
  407.3 2.7 reshape.87
  410.0 593.5 %while.32 = (s32[]{:T(128)}, f32[48,256]{1,0:T(8,128)S(1)}, f32[192,256]{1,0:T(8,128)S(1)}, s32[]{:T(128)}, f32[192,2048]{1,0:T(8,128)}, /*index=5*/f32[2048,256...) while((s32[]{:T(128)}, f32[48,256]{1,0:T(8,128)S(1)}, ...), condition=%wide.region_10.11_spmd, body=%wide.region_8.10_spmd.sunk | while | flops 604286976 | bytes 8521536 | solution.py:26
  410.1 5.6 collective-permute-start
  416.5 3.8 convolution_subtract_fusion.2
  420.3 74.7 %all-reduce.3.cloned.1.call-done = f32[48,2048]{1,0:T(8,128)} async-done(((f32[48,2048]{1,0:T(8,128)}), f32[48,2048]{1,0:T(8,128)}) %all-reduce.3.cloned.1.call-update) | async-done | bytes 393232 | tf_op jit(solution)/shard_map/while/body/eval_jaxpr/psum | solution.py:22
  495.1 3.8 select_dynamic-update-slice_fusion.4
  501.1 3.8 convolution_subtract_fusion.2
  505.0 74.2 %all-reduce.3.cloned.1.call-done = f32[48,2048]{1,0:T(8,128)} async-done(((f32[48,2048]{1,0:T(8,128)}), f32[48,2048]{1,0:T(8,128)}) %all-reduce.3.cloned.1.call-update) | async-done | bytes 393232 | tf_op jit(solution)/shard_map/while/body/eval_jaxpr/psum | solution.py:22
  579.2 3.8 select_dynamic-update-slice_fusion.4
  585.3 3.8 convolution_subtract_fusion.2
  589.1 74.2 %all-reduce.3.cloned.1.call-done = f32[48,2048]{1,0:T(8,128)} async-done(((f32[48,2048]{1,0:T(8,128)}), f32[48,2048]{1,0:T(8,128)}) %all-reduce.3.cloned.1.call-update) | async-done | bytes 393232 | tf_op jit(solution)/shard_map/while/body/eval_jaxpr/psum | solution.py:22
  663.3 3.8 select_dynamic-update-slice_fusion.4
  669.4 3.8 convolution_subtract_fusion.2
  673.2 74.2 %all-reduce.3.cloned.1.call-done = f32[48,2048]{1,0:T(8,128)} async-done(((f32[48,2048]{1,0:T(8,128)}), f32[48,2048]{1,0:T(8,128)}) %all-reduce.3.cloned.1.call-update) | async-done | bytes 393232 | tf_op jit(solution)/shard_map/while/body/eval_jaxpr/psum | solution.py:22
  747.4 3.8 select_dynamic-update-slice_fusion.4
  751.3 1.3 collective-permute-start
  753.5 3.8 convolution_subtract_fusion.2
  757.3 74.2 %all-reduce.3.cloned.1.call-done = f32[48,2048]{1,0:T(8,128)} async-done(((f32[48,2048]{1,0:T(8,128)}), f32[48,2048]{1,0:T(8,128)}) %all-reduce.3.cloned.1.call-update) | async-done | bytes 393232 | tf_op jit(solution)/shard_map/while/body/eval_jaxpr/psum | solution.py:22
  831.5 3.8 select_dynamic-update-slice_fusion.4
  837.6 3.8 convolution_subtract_fusion.2
  841.4 74.2 %all-reduce.3.cloned.1.call-done = f32[48,2048]{1,0:T(8,128)} async-done(((f32[48,2048]{1,0:T(8,128)}), f32[48,2048]{1,0:T(8,128)}) %all-reduce.3.cloned.1.call-update) | async-done | bytes 393232 | tf_op jit(solution)/shard_map/while/body/eval_jaxpr/psum | solution.py:22
  915.6 3.8 select_dynamic-update-slice_fusion.4
  921.7 3.8 convolution_subtract_fusion.2
  925.5 74.2 %all-reduce.3.cloned.1.call-done = f32[48,2048]{1,0:T(8,128)} async-done(((f32[48,2048]{1,0:T(8,128)}), f32[48,2048]{1,0:T(8,128)}) %all-reduce.3.cloned.1.call-update) | async-done | bytes 393232 | tf_op jit(solution)/shard_map/while/body/eval_jaxpr/psum | solution.py:22
  999.7 3.8 select_dynamic-update-slice_fusion.4
  1003.6 571.6 %while.33 = (s32[]{:T(128)}, f32[48,256]{1,0:T(8,128)S(1)}, f32[192,256]{1,0:T(8,128)S(1)}, s32[]{:T(128)}, f32[192,256]{1,0:T(8,128)S(1)}, /*index=5*/f32[256,2...) while((s32[]{:T(128)}, f32[48,256]{1,0:T(8,128)S(1)}, ...), condition=%wide.region_13.14_spmd, body=%wide.region_11.13_spmd.sunk | while | flops 604102656 | bytes 7831881 | solution.py:26
  1005.0 1.8 collective-permute-done.1
  1006.8 3.7 fusion.42
  1010.5 71.8 %all-reduce.5.cloned.1.call-done = f32[48,2048]{1,0:T(8,128)} async-done(((f32[48,2048]{1,0:T(8,128)}), f32[48,2048]{1,0:T(8,128)}) %all-reduce.5.cloned.1.call-update) | async-done | bytes 393232 | tf_op jit(solution)/shard_map/while/body/eval_jaxpr/psum | solution.py:22
  1082.3 2.1 fusion.43
  1086.6 1.8 collective-permute-done.1
  1088.4 3.7 fusion.42
  1092.1 71.9 %all-reduce.5.cloned.1.call-done = f32[48,2048]{1,0:T(8,128)} async-done(((f32[48,2048]{1,0:T(8,128)}), f32[48,2048]{1,0:T(8,128)}) %all-reduce.5.cloned.1.call-update) | async-done | bytes 393232 | tf_op jit(solution)/shard_map/while/body/eval_jaxpr/psum | solution.py:22
  1164.0 2.1 fusion.43
  1168.3 1.8 collective-permute-done.1
  1170.1 3.7 fusion.42
  1173.8 71.8 %all-reduce.5.cloned.1.call-done = f32[48,2048]{1,0:T(8,128)} async-done(((f32[48,2048]{1,0:T(8,128)}), f32[48,2048]{1,0:T(8,128)}) %all-reduce.5.cloned.1.call-update) | async-done | bytes 393232 | tf_op jit(solution)/shard_map/while/body/eval_jaxpr/psum | solution.py:22
  1245.7 2.1 fusion.43
  1249.9 1.8 collective-permute-done.1
  1251.8 3.7 fusion.42
  1255.5 71.8 %all-reduce.5.cloned.1.call-done = f32[48,2048]{1,0:T(8,128)} async-done(((f32[48,2048]{1,0:T(8,128)}), f32[48,2048]{1,0:T(8,128)}) %all-reduce.5.cloned.1.call-update) | async-done | bytes 393232 | tf_op jit(solution)/shard_map/while/body/eval_jaxpr/psum | solution.py:22
  1327.3 2.1 fusion.43
  1331.6 1.8 collective-permute-done.1
  1333.4 3.7 fusion.42
  1337.1 71.8 %all-reduce.5.cloned.1.call-done = f32[48,2048]{1,0:T(8,128)} async-done(((f32[48,2048]{1,0:T(8,128)}), f32[48,2048]{1,0:T(8,128)}) %all-reduce.5.cloned.1.call-update) | async-done | bytes 393232 | tf_op jit(solution)/shard_map/while/body/eval_jaxpr/psum | solution.py:22
  1409.0 2.1 fusion.43
  1413.2 1.8 collective-permute-done.1
  1415.1 3.7 fusion.42
  1418.8 71.8 %all-reduce.5.cloned.1.call-done = f32[48,2048]{1,0:T(8,128)} async-done(((f32[48,2048]{1,0:T(8,128)}), f32[48,2048]{1,0:T(8,128)}) %all-reduce.5.cloned.1.call-update) | async-done | bytes 393232 | tf_op jit(solution)/shard_map/while/body/eval_jaxpr/psum | solution.py:22
  1490.6 2.1 fusion.43
  1494.9 1.8 collective-permute-done.1
  1496.7 3.7 fusion.42
  1500.4 71.8 %all-reduce.5.cloned.1.call-done = f32[48,2048]{1,0:T(8,128)} async-done(((f32[48,2048]{1,0:T(8,128)}), f32[48,2048]{1,0:T(8,128)}) %all-reduce.5.cloned.1.call-update) | async-done | bytes 393232 | tf_op jit(solution)/shard_map/while/body/eval_jaxpr/psum | solution.py:22
  1572.3 2.1 fusion.43
  (101 shorter events, 34.8 us)
Async XLA Ops:
  78.8 68.7 %copy-start.1 = (f32[24,24,512]{2,1,0:T(8,128)S(1)}, f32[24,24,512]{2,1,0:T(8,128)}, u32[]{:S(2)}) copy-start(f32[24,24,512]{2,1,0:T(8,128)} %param.16) | copy-start | bytes 3538948
  78.8 68.7 %copy-start.2 = (f32[24,24,512]{2,1,0:T(8,128)S(1)}, f32[24,24,512]{2,1,0:T(8,128)}, u32[]{:S(2)}) copy-start(f32[24,24,512]{2,1,0:T(8,128)} %param.17) | copy-start | bytes 3538948
  146.8 1.2 copy-start.4
  149.9 29.1 %copy-start.7 = (s32[512]{0:T(512)S(1)}, s32[512]{0:T(512)}, u32[]{:S(2)}) copy-start(s32[512]{0:T(512)} %param.20) | copy-start | bytes 6148
  175.5 70.0 %copy-start.5 = (f32[2048]{0:T(1024)S(1)}, f32[2048]{0:T(1024)}, u32[]{:S(2)}) copy-start(f32[2048]{0:T(1024)} %param.22) | copy-start | bytes 24580
  175.5 66.4 %all-to-all-start.1 = ((f32[4,24,256]{2,1,0:T(8,128)}), f32[4,24,256]{2,1,0:T(8,128)S(1)}, u32[]{:S(2)}, u32[]{:S(2)}) async-start(f32[4,24,256]{2,1,0:T(8,128)} %copy.20), calls=%async_computation.1 | async-start | bytes 196608 | tf_op jit(solution)/shard_map/all_to_all | solution.py:75
  242.0 165.3 %copy-start.6 = (f32[192]{0:T(256)}, f32[192]{0:T(256)S(1)}, u32[]{:S(2)}) copy-start(f32[192]{0:T(256)S(1)} %psum.31) | copy-start | bytes 2308
  242.0 7.8 all-to-all-start
  407.3 2.7 copy-start
  410.0 85.1 %all-reduce.3.cloned.1.call-start = ((), (), s32[]{:S(2)}) async-start(), calls=%async_computation.2 | async-start | bytes 786432 | tf_op jit(solution)/shard_map/while/body/eval_jaxpr/psum | solution.py:22
  410.1 6.4 collective-permute-start
  498.9 80.2 %all-reduce.3.cloned.1.call-start = ((), (), s32[]{:S(2)}) async-start(), calls=%async_computation.2 | async-start | bytes 786432 | tf_op jit(solution)/shard_map/while/body/eval_jaxpr/psum | solution.py:22
  499.0 2.2 collective-permute-start
  583.0 80.3 %all-reduce.3.cloned.1.call-start = ((), (), s32[]{:S(2)}) async-start(), calls=%async_computation.2 | async-start | bytes 786432 | tf_op jit(solution)/shard_map/while/body/eval_jaxpr/psum | solution.py:22
  583.1 2.2 collective-permute-start
  667.2 80.2 %all-reduce.3.cloned.1.call-start = ((), (), s32[]{:S(2)}) async-start(), calls=%async_computation.2 | async-start | bytes 786432 | tf_op jit(solution)/shard_map/while/body/eval_jaxpr/psum | solution.py:22
  667.2 2.2 collective-permute-start
  751.3 80.2 %all-reduce.3.cloned.1.call-start = ((), (), s32[]{:S(2)}) async-start(), calls=%async_computation.2 | async-start | bytes 786432 | tf_op jit(solution)/shard_map/while/body/eval_jaxpr/psum | solution.py:22
  751.3 2.2 collective-permute-start
  835.4 80.2 %all-reduce.3.cloned.1.call-start = ((), (), s32[]{:S(2)}) async-start(), calls=%async_computation.2 | async-start | bytes 786432 | tf_op jit(solution)/shard_map/while/body/eval_jaxpr/psum | solution.py:22
  835.4 2.2 collective-permute-start
  919.5 80.2 %all-reduce.3.cloned.1.call-start = ((), (), s32[]{:S(2)}) async-start(), calls=%async_computation.2 | async-start | bytes 786432 | tf_op jit(solution)/shard_map/while/body/eval_jaxpr/psum | solution.py:22
  919.5 2.2 collective-permute-start
  1003.6 78.7 %all-reduce.5.cloned.1.call-start = ((), (), s32[]{:S(2)}) async-start(), calls=%async_computation.3 | async-start | bytes 786432 | tf_op jit(solution)/shard_map/while/body/eval_jaxpr/psum | solution.py:22
  1003.7 3.1 collective-permute-start.1
  1085.3 78.7 %all-reduce.5.cloned.1.call-start = ((), (), s32[]{:S(2)}) async-start(), calls=%async_computation.3 | async-start | bytes 786432 | tf_op jit(solution)/shard_map/while/body/eval_jaxpr/psum | solution.py:22
  1085.3 3.1 collective-permute-start.1
  1166.9 78.7 %all-reduce.5.cloned.1.call-start = ((), (), s32[]{:S(2)}) async-start(), calls=%async_computation.3 | async-start | bytes 786432 | tf_op jit(solution)/shard_map/while/body/eval_jaxpr/psum | solution.py:22
  1167.0 3.1 collective-permute-start.1
  1248.6 78.7 %all-reduce.5.cloned.1.call-start = ((), (), s32[]{:S(2)}) async-start(), calls=%async_computation.3 | async-start | bytes 786432 | tf_op jit(solution)/shard_map/while/body/eval_jaxpr/psum | solution.py:22
  1248.6 3.1 collective-permute-start.1
  1330.2 78.7 %all-reduce.5.cloned.1.call-start = ((), (), s32[]{:S(2)}) async-start(), calls=%async_computation.3 | async-start | bytes 786432 | tf_op jit(solution)/shard_map/while/body/eval_jaxpr/psum | solution.py:22
  1330.3 3.1 collective-permute-start.1
  1411.9 78.7 %all-reduce.5.cloned.1.call-start = ((), (), s32[]{:S(2)}) async-start(), calls=%async_computation.3 | async-start | bytes 786432 | tf_op jit(solution)/shard_map/while/body/eval_jaxpr/psum | solution.py:22
  1411.9 3.1 collective-permute-start.1
  1493.5 78.7 %all-reduce.5.cloned.1.call-start = ((), (), s32[]{:S(2)}) async-start(), calls=%async_computation.3 | async-start | bytes 786432 | tf_op jit(solution)/shard_map/while/body/eval_jaxpr/psum | solution.py:22
  1493.6 3.1 collective-permute-start.1
  1575.2 0.7 copy-start.3
Sparse Core Ops, SparseCore 0:
  420.4 74.5 all-reduce.2
  505.1 74.0 all-reduce.2
  589.2 74.0 all-reduce.2
  673.3 74.0 all-reduce.2
  757.4 74.0 all-reduce.2
  841.5 74.0 all-reduce.2
  925.6 74.0 all-reduce.2
  1010.6 71.6 all-reduce.4
  1092.3 71.6 all-reduce.4
  1173.9 71.6 all-reduce.4
  1255.6 71.6 all-reduce.4
  1337.2 71.6 all-reduce.4
  1418.9 71.6 all-reduce.4
  1500.5 71.6 all-reduce.4
where the time goes:
time: 1580 us
  waiting for transfers between devices  1040 us (66%)
  other arithmetic  168 us (11%)
  local copies, waits for them, and re-layouts  123 us (8%)
  blocking collectives  107 us (7%)
  matrix products  94.3 us (6%)
  starting transfers between devices  29.9 us (2%)
    psum x14, waiting for transfers between devices, advance(): summed = lax.psum(partial_value, 'band')  1020 us
    scatter-add x1, other arithmetic, on_device(): assembled = jnp.zeros((VARS * slab_rows,), jnp.float32).at[got_index.resh...  157 us
    all_gather x1, blocking collectives, on_device(): whole_mode = lax.all_gather(mode, ('chain', 'band'), axis=0, tiled=True)  70.1 us
    gather x2, local copies, waits for them, and re-layouts, on_device(): mode_at = whole_mode[dof_index]  68 us
    psum x1, blocking collectives, on_device(): eigval_slope = lax.psum(local_slope, ('chain', 'band'))  36.8 us
  transfers between devices with their start and end apart: 30, of which 29 were waited for; matrix products, arithmetic and copies ran while one was open for 2% of the time, Pallas kernels for 0%

commit v1 on v0

--- a/solution.py
+++ b/solution.py
@@ -5,6 +5,11 @@
 
 VARS = 192
 PANELS = 4
+
+
+def see_points_on(x0, shard_axis):
+    x_next = jnp.sum(jax.lax.all_gather(x0, axis_name=shard_axis), 0)
+    return x_next
 
 
 def from_behind(value, axis, by):
@@ -19,7 +24,7 @@
         outgoing, kept = carry
         received = from_behind(outgoing, "chain", shift_by)
         partial_value, context = prepare(iteration, received, kept)
-        summed = lax.psum(partial_value, "band")
+        summed = see_points_on(partial_value, "band")
         return finish(iteration, summed, context, kept)
 
     outgoing = jnp.zeros((panel_rows, piece_cols), jnp.float32)

time: 1580 us -> 1430 us (0.905)
  waiting for transfers between devices: 1040 us -> 875 us
  other arithmetic: 168 us -> 191 us
    psum x14 -> x0, waiting for transfers between devices: 1020 us -> none  [advance(): summed = lax.psum(partial_value, 'band')]
    all_gather x0 -> x14, waiting for transfers between devices: none -> 853 us  [see_points_on(): x_next = jnp.sum(jax.lax.all_gather(x0, axis_name=shard_axis), 0)]
    reduce_sum x0 -> x14, other arithmetic: none -> 29.2 us  [see_points_on(): x_next = jnp.sum(jax.lax.all_gather(x0, axis_name=shard_axis), 0)]
where the time goes in v1:
time: 1430 us
  waiting for transfers between devices  875 us (61%)
  other arithmetic  191 us (13%)
  local copies, waits for them, and re-layouts  124 us (9%)
  blocking collectives  107 us (7%)
  matrix products  86.7 us (6%)
  starting transfers between devices  29.9 us (2%)
  between operations  14.6 us (1%)
    all_gather x14, waiting for transfers between devices, see_points_on(): x_next = jnp.sum(jax.lax.all_gather(x0, axis_name=shard_axis), 0)  853 us
    scatter-add x1, other arithmetic, on_device(): assembled = jnp.zeros((VARS * slab_rows,), jnp.float32).at[got_index.resh...  157 us
    all_gather x1, blocking collectives, on_device(): whole_mode = lax.all_gather(mode, ('chain', 'band'), axis=0, tiled=True)  70.1 us
    gather x2, local copies, waits for them, and re-layouts, on_device(): mode_at = whole_mode[dof_index]  68 us
    psum x1, blocking collectives, on_device(): eigval_slope = lax.psum(local_slope, ('chain', 'band'))  36.8 us
    reduce_sum x14, other arithmetic, see_points_on(): x_next = jnp.sum(jax.lax.all_gather(x0, axis_name=shard_axis), 0)  29.2 us
  transfers between devices with their start and end apart: 30, of which 29 were waited for; matrix products, arithmetic and copies ran while one was open for 2% of the time, Pallas kernels for 0%

profile of v1, /device:TPU:0, one launch (start us, length us, event | category | flops | bytes accessed | tf_op | source)
XLA Modules:
  0.0 1429.3 jit_solution(11021643182220738510)
XLA Ops:
  8.7 70.1 %all-gather.2 = f32[32,1,256]{2,1,0:T(1,128)S(1)} all-gather(f32[1,1,256]{2,1,0:T(1,128)} %bitcast.81), channel_id=1, replica_groups=mesh['chain'=4,'band'=8] {'chain','band'}, dimensions={0}, use_global_device_ids=true | all-gather | bytes 33792 | tf_op jit(solution)/shard_map/all_gather | solution.py:56
  78.8 68.0 %gather_fusion = f32[12288]{0:T(1024)S(1)} fusion(f32[8192]{0:T(1024)S(1)} %bitcast.65, s32[12288]{0:T(1024)S(1)} %broadcast_clamp_fusion), kind=kCustom, calls=%fused_computation | custom fusion | bytes 147456 | tf_op jit(solution)/shard_map/gather | solution.py:59
  149.9 24.8 %scatter_fusion.1 = f32[4,24,256]{1,2,0:T(8,128)S(1)} fusion(f32[4,24,256]{1,2,0:T(8,128)S(1)} %broadcast_in_dim.10, s32[512]{0:T(512)S(1)} %bitcast.66, f32[512,24]{1,0:T(8,128)S(1)} %copy.19), kind=kCustom, calls=%fused_computation.2 | custom fusion | bytes 151552 | tf_op jit(solution)/shard_map/scatter | solution.py:72
  175.5 3.4 all-to-all-start.1
  179.5 24.8 %scatter_fusion = s32[4,24,256]{1,2,0:T(8,128)S(1)} fusion(s32[4,24,256]{1,2,0:T(8,128)S(1)} %broadcast_in_dim.9, s32[512]{0:T(512)S(1)} %bitcast.67, s32[512,24]{1,0:T(8,128)S(1)} %copy.17), kind=kCustom, calls=%fused_computation.1 | custom fusion | bytes 151552 | tf_op jit(solution)/shard_map/scatter | solution.py:77
  205.2 36.8 %psum.7 = f32[192]{0:T(256)S(1)} all-reduce(f32[192]{0:T(256)S(1)} %bitcast.82), channel_id=1, replica_groups=mesh['chain'=4,'band'=8] {'chain','band'}, use_global_device_ids=true, to_apply=%region_7.8 | all-reduce | flops 192 | bytes 1536 | tf_op jit(solution)/shard_map/psum | solution.py:65
  242.0 3.5 all-to-all-start
  246.9 2.9 all-to-all-done
  250.0 157.3 %scatter_custom_fusion.2 = f32[393216]{0:T(1024)} fusion(s32[24576]{0:T(1024)S(1)} %bitcast.74, f32[24576]{0:T(1024)S(1)} %bitcast.73, f32[]{:T(128)} %constant.153.clone.1), kind=kCustom, calls=%fused_computation.17 | custom fusion | flops 24576 | bytes 1572868 | tf_op jit(solution)/shard_map/scatter-add | solution.py:86
  407.3 2.7 reshape.87
  410.1 523.1 %while.32 = (s32[]{:T(128)}, f32[48,256]{1,0:T(8,128)S(1)}, f32[192,256]{1,0:T(8,128)S(1)}, s32[]{:T(128)}, f32[192,2048]{1,0:T(8,128)}, /*index=5*/f32[2048,256...) while((s32[]{:T(128)}, f32[48,256]{1,0:T(8,128)S(1)}, ...), condition=%wide.region_10.11_spmd, body=%wide.region_8.10_spmd.sunk | while | flops 604876800 | bytes 20318028 | solution.py:31
  410.1 5.6 collective-permute-start
  416.6 3.8 convolution_subtract_fusion.2
  420.4 63.0 %all-gather.10.cloned.1.call-done = f32[384,2048]{1,0:T(8,128)} async-done(((f32[48,2048]{1,0:T(8,128)}), f32[384,2048]{1,0:T(8,128)}) %all-gather.10.cloned.1.call-update) | async-done | bytes 3145744 | tf_op jit(solution)/shard_map/while/body/eval_jaxpr/all_gather | solution.py:11
  483.4 2.1 reduce_sum.55
  485.5 3.7 select_dynamic-update-slice_fusion.4
  491.5 3.8 convolution_subtract_fusion.2
  495.3 62.1 %all-gather.10.cloned.1.call-done = f32[384,2048]{1,0:T(8,128)} async-done(((f32[48,2048]{1,0:T(8,128)}), f32[384,2048]{1,0:T(8,128)}) %all-gather.10.cloned.1.call-update) | async-done | bytes 3145744 | tf_op jit(solution)/shard_map/while/body/eval_jaxpr/all_gather | solution.py:11
  557.4 2.1 reduce_sum.55
  559.5 3.7 select_dynamic-update-slice_fusion.4
  565.5 3.8 convolution_subtract_fusion.2
  569.3 62.1 %all-gather.10.cloned.1.call-done = f32[384,2048]{1,0:T(8,128)} async-done(((f32[48,2048]{1,0:T(8,128)}), f32[384,2048]{1,0:T(8,128)}) %all-gather.10.cloned.1.call-update) | async-done | bytes 3145744 | tf_op jit(solution)/shard_map/while/body/eval_jaxpr/all_gather | solution.py:11
  631.4 2.1 reduce_sum.55
  633.5 3.7 select_dynamic-update-slice_fusion.4
  639.4 3.8 convolution_subtract_fusion.2
  643.3 62.1 %all-gather.10.cloned.1.call-done = f32[384,2048]{1,0:T(8,128)} async-done(((f32[48,2048]{1,0:T(8,128)}), f32[384,2048]{1,0:T(8,128)}) %all-gather.10.cloned.1.call-update) | async-done | bytes 3145744 | tf_op jit(solution)/shard_map/while/body/eval_jaxpr/all_gather | solution.py:11
  705.4 2.1 reduce_sum.55
  707.5 3.7 select_dynamic-update-slice_fusion.4
  713.4 3.8 convolution_subtract_fusion.2
  717.3 62.1 %all-gather.10.cloned.1.call-done = f32[384,2048]{1,0:T(8,128)} async-done(((f32[48,2048]{1,0:T(8,128)}), f32[384,2048]{1,0:T(8,128)}) %all-gather.10.cloned.1.call-update) | async-done | bytes 3145744 | tf_op jit(solution)/shard_map/while/body/eval_jaxpr/all_gather | solution.py:11
  779.4 2.1 reduce_sum.55
  781.5 3.7 select_dynamic-update-slice_fusion.4
  787.4 3.8 convolution_subtract_fusion.2
  791.3 62.1 %all-gather.10.cloned.1.call-done = f32[384,2048]{1,0:T(8,128)} async-done(((f32[48,2048]{1,0:T(8,128)}), f32[384,2048]{1,0:T(8,128)}) %all-gather.10.cloned.1.call-update) | async-done | bytes 3145744 | tf_op jit(solution)/shard_map/while/body/eval_jaxpr/all_gather | solution.py:11
  853.4 2.1 reduce_sum.55
  855.4 3.7 select_dynamic-update-slice_fusion.4
  861.4 3.8 convolution_subtract_fusion.2
  865.3 62.1 %all-gather.10.cloned.1.call-done = f32[384,2048]{1,0:T(8,128)} async-done(((f32[48,2048]{1,0:T(8,128)}), f32[384,2048]{1,0:T(8,128)}) %all-gather.10.cloned.1.call-update) | async-done | bytes 3145744 | tf_op jit(solution)/shard_map/while/body/eval_jaxpr/all_gather | solution.py:11
  927.3 2.1 reduce_sum.55
  929.4 3.7 select_dynamic-update-slice_fusion.4
  933.2 488.9 %while.33 = (s32[]{:T(128)}, f32[48,256]{1,0:T(8,128)S(1)}, f32[192,256]{1,0:T(8,128)S(1)}, s32[]{:T(128)}, f32[192,256]{1,0:T(8,128)S(1)}, /*index=5*/f32[256,2...) while((s32[]{:T(128)}, f32[48,256]{1,0:T(8,128)S(1)}, ...), condition=%wide.region_13.14_spmd, body=%wide.region_11.13_spmd.sunk | while | flops 604692480 | bytes 19628372 | solution.py:31
  934.6 1.8 collective-permute-done.1
  936.4 3.7 fusion.42
  940.1 59.7 %all-gather.12.cloned.1.call-done = f32[384,2048]{1,0:T(8,128)} async-done(((f32[48,2048]{1,0:T(8,128)}), f32[384,2048]{1,0:T(8,128)}) %all-gather.12.cloned.1.call-update) | async-done | bytes 3145744 | tf_op jit(solution)/shard_map/while/body/eval_jaxpr/all_gather | solution.py:11
  999.8 2.1 reduce_sum.56
  1004.4 1.8 collective-permute-done.1
  1006.2 3.7 fusion.42
  1010.0 59.7 %all-gather.12.cloned.1.call-done = f32[384,2048]{1,0:T(8,128)} async-done(((f32[48,2048]{1,0:T(8,128)}), f32[384,2048]{1,0:T(8,128)}) %all-gather.12.cloned.1.call-update) | async-done | bytes 3145744 | tf_op jit(solution)/shard_map/while/body/eval_jaxpr/all_gather | solution.py:11
  1069.7 2.1 reduce_sum.56
  1076.1 3.7 fusion.42
  1079.8 59.7 %all-gather.12.cloned.1.call-done = f32[384,2048]{1,0:T(8,128)} async-done(((f32[48,2048]{1,0:T(8,128)}), f32[384,2048]{1,0:T(8,128)}) %all-gather.12.cloned.1.call-update) | async-done | bytes 3145744 | tf_op jit(solution)/shard_map/while/body/eval_jaxpr/all_gather | solution.py:11
  1139.5 2.1 reduce_sum.56
  1145.9 3.7 fusion.42
  1149.6 59.7 %all-gather.12.cloned.1.call-done = f32[384,2048]{1,0:T(8,128)} async-done(((f32[48,2048]{1,0:T(8,128)}), f32[384,2048]{1,0:T(8,128)}) %all-gather.12.cloned.1.call-update) | async-done | bytes 3145744 | tf_op jit(solution)/shard_map/while/body/eval_jaxpr/all_gather | solution.py:11
  1209.3 2.1 reduce_sum.56
  1215.8 3.7 fusion.42
  1219.5 59.7 %all-gather.12.cloned.1.call-done = f32[384,2048]{1,0:T(8,128)} async-done(((f32[48,2048]{1,0:T(8,128)}), f32[384,2048]{1,0:T(8,128)}) %all-gather.12.cloned.1.call-update) | async-done | bytes 3145744 | tf_op jit(solution)/shard_map/while/body/eval_jaxpr/all_gather | solution.py:11
  1279.2 2.1 reduce_sum.56
  1285.6 3.7 fusion.42
  1289.3 59.7 %all-gather.12.cloned.1.call-done = f32[384,2048]{1,0:T(8,128)} async-done(((f32[48,2048]{1,0:T(8,128)}), f32[384,2048]{1,0:T(8,128)}) %all-gather.12.cloned.1.call-update) | async-done | bytes 3145744 | tf_op jit(solution)/shard_map/while/body/eval_jaxpr/all_gather | solution.py:11
  1349.0 2.1 reduce_sum.56
  1355.5 3.7 fusion.42
  1359.2 59.7 %all-gather.12.cloned.1.call-done = f32[384,2048]{1,0:T(8,128)} async-done(((f32[48,2048]{1,0:T(8,128)}), f32[384,2048]{1,0:T(8,128)}) %all-gather.12.cloned.1.call-update) | async-done | bytes 3145744 | tf_op jit(solution)/shard_map/while/body/eval_jaxpr/all_gather | solution.py:11
  1418.9 2.1 reduce_sum.56
  (115 shorter events, 48.7 us)
Async XLA Ops:
  78.8 68.7 %copy-start.1 = (f32[24,24,512]{2,1,0:T(8,128)S(1)}, f32[24,24,512]{2,1,0:T(8,128)}, u32[]{:S(2)}) copy-start(f32[24,24,512]{2,1,0:T(8,128)} %param.16) | copy-start | bytes 3538948
  78.8 68.7 %copy-start.2 = (f32[24,24,512]{2,1,0:T(8,128)S(1)}, f32[24,24,512]{2,1,0:T(8,128)}, u32[]{:S(2)}) copy-start(f32[24,24,512]{2,1,0:T(8,128)} %param.17) | copy-start | bytes 3538948
  146.8 1.2 copy-start.4
  149.9 29.1 %copy-start.7 = (s32[512]{0:T(512)S(1)}, s32[512]{0:T(512)}, u32[]{:S(2)}) copy-start(s32[512]{0:T(512)} %param.20) | copy-start | bytes 6148
  175.5 70.0 %copy-start.5 = (f32[2048]{0:T(1024)S(1)}, f32[2048]{0:T(1024)}, u32[]{:S(2)}) copy-start(f32[2048]{0:T(1024)} %param.22) | copy-start | bytes 24580
  175.5 66.4 %all-to-all-start.1 = ((f32[4,24,256]{2,1,0:T(8,128)}), f32[4,24,256]{2,1,0:T(8,128)S(1)}, u32[]{:S(2)}, u32[]{:S(2)}) async-start(f32[4,24,256]{2,1,0:T(8,128)} %copy.20), calls=%async_computation.1 | async-start | bytes 196608 | tf_op jit(solution)/shard_map/all_to_all | solution.py:80
  242.0 165.3 %copy-start.6 = (f32[192]{0:T(256)}, f32[192]{0:T(256)S(1)}, u32[]{:S(2)}) copy-start(f32[192]{0:T(256)S(1)} %psum.7) | copy-start | bytes 2308
  242.0 7.8 all-to-all-start
  407.3 2.7 copy-start
  410.1 73.3 %all-gather.10.cloned.1.call-start = ((), (), s32[]{:S(2)}) async-start(), calls=%async_computation.2 | async-start | bytes 3538944 | tf_op jit(solution)/shard_map/while/body/eval_jaxpr/all_gather | solution.py:11
  410.1 6.4 collective-permute-start
  489.3 68.1 %all-gather.10.cloned.1.call-start = ((), (), s32[]{:S(2)}) async-start(), calls=%async_computation.2 | async-start | bytes 3538944 | tf_op jit(solution)/shard_map/while/body/eval_jaxpr/all_gather | solution.py:11
  489.3 2.2 collective-permute-start
  563.2 68.1 %all-gather.10.cloned.1.call-start = ((), (), s32[]{:S(2)}) async-start(), calls=%async_computation.2 | async-start | bytes 3538944 | tf_op jit(solution)/shard_map/while/body/eval_jaxpr/all_gather | solution.py:11
  563.3 2.2 collective-permute-start
  637.2 68.1 %all-gather.10.cloned.1.call-start = ((), (), s32[]{:S(2)}) async-start(), calls=%async_computation.2 | async-start | bytes 3538944 | tf_op jit(solution)/shard_map/while/body/eval_jaxpr/all_gather | solution.py:11
  637.3 2.2 collective-permute-start
  711.2 68.1 %all-gather.10.cloned.1.call-start = ((), (), s32[]{:S(2)}) async-start(), calls=%async_computation.2 | async-start | bytes 3538944 | tf_op jit(solution)/shard_map/while/body/eval_jaxpr/all_gather | solution.py:11
  711.3 2.2 collective-permute-start
  785.2 68.1 %all-gather.10.cloned.1.call-start = ((), (), s32[]{:S(2)}) async-start(), calls=%async_computation.2 | async-start | bytes 3538944 | tf_op jit(solution)/shard_map/while/body/eval_jaxpr/all_gather | solution.py:11
  785.3 2.2 collective-permute-start
  859.2 68.1 %all-gather.10.cloned.1.call-start = ((), (), s32[]{:S(2)}) async-start(), calls=%async_computation.2 | async-start | bytes 3538944 | tf_op jit(solution)/shard_map/while/body/eval_jaxpr/all_gather | solution.py:11
  859.2 2.2 collective-permute-start
  933.2 66.6 %all-gather.12.cloned.1.call-start = ((), (), s32[]{:S(2)}) async-start(), calls=%async_computation.3 | async-start | bytes 3538944 | tf_op jit(solution)/shard_map/while/body/eval_jaxpr/all_gather | solution.py:11
  933.3 3.1 collective-permute-start.1
  1003.1 66.6 %all-gather.12.cloned.1.call-start = ((), (), s32[]{:S(2)}) async-start(), calls=%async_computation.3 | async-start | bytes 3538944 | tf_op jit(solution)/shard_map/while/body/eval_jaxpr/all_gather | solution.py:11
  1003.1 3.1 collective-permute-start.1
  1072.9 66.6 %all-gather.12.cloned.1.call-start = ((), (), s32[]{:S(2)}) async-start(), calls=%async_computation.3 | async-start | bytes 3538944 | tf_op jit(solution)/shard_map/while/body/eval_jaxpr/all_gather | solution.py:11
  1073.0 3.1 collective-permute-start.1
  1142.8 66.6 %all-gather.12.cloned.1.call-start = ((), (), s32[]{:S(2)}) async-start(), calls=%async_computation.3 | async-start | bytes 3538944 | tf_op jit(solution)/shard_map/while/body/eval_jaxpr/all_gather | solution.py:11
  1142.8 3.1 collective-permute-start.1
  1212.6 66.6 %all-gather.12.cloned.1.call-start = ((), (), s32[]{:S(2)}) async-start(), calls=%async_computation.3 | async-start | bytes 3538944 | tf_op jit(solution)/shard_map/while/body/eval_jaxpr/all_gather | solution.py:11
  1212.7 3.1 collective-permute-start.1
  1282.4 66.6 %all-gather.12.cloned.1.call-start = ((), (), s32[]{:S(2)}) async-start(), calls=%async_computation.3 | async-start | bytes 3538944 | tf_op jit(solution)/shard_map/while/body/eval_jaxpr/all_gather | solution.py:11
  1282.5 3.1 collective-permute-start.1
  1352.3 66.6 %all-gather.12.cloned.1.call-start = ((), (), s32[]{:S(2)}) async-start(), calls=%async_computation.3 | async-start | bytes 3538944 | tf_op jit(solution)/shard_map/while/body/eval_jaxpr/all_gather | solution.py:11
  1352.3 3.1 collective-permute-start.1
  1422.1 0.7 copy-start.3
Sparse Core Ops, SparseCore 0:
  420.5 62.8 all-gather.9
  495.4 61.9 all-gather.9
  569.4 61.9 all-gather.9
  643.4 61.9 all-gather.9
  717.4 61.9 all-gather.9
  791.4 61.9 all-gather.9
  865.4 61.9 all-gather.9
  940.2 59.5 all-gather.11
  1010.1 59.5 all-gather.11
  1079.9 59.5 all-gather.11
  1149.8 59.5 all-gather.11
  1219.6 59.5 all-gather.11
  1289.4 59.5 all-gather.11
  1359.3 59.5 all-gather.11
